TPU v7x, 32 devices: a whole 2x2x4 slice. The times are simulated.
32 devices in a mesh: dp: 8 (over y, x, core), tensor: 4 (over z).
Axes of the slice: x: 2, y: 2, z: 4, core: 2. Of those that a mesh axis runs over, the one named last changes fastest.
Arguments:
- tokens: bfloat16 [32, 1024, 512], P(('dp', 'tensor')), may hold values from -6 to 6
- timestep: int32 [32], P(('dp', 'tensor')), may hold values from 0 to 999
- segment_ids: int32 [32, 1024], P('dp'), may hold values from 0 to 7, never falling along the last dimension, each value on 1 to 512 neighbouring positions
- span_lengths: int32 [32], P('dp'), may hold values from 512 to 1024
- w_qkv: float32 [3, 512, 512], P(None, 'dp', 'tensor'), may hold values from -0.25 to 0.25
- w_out_t: float32 [512, 512], P('dp', 'tensor'), may hold values from -1.5 to 1.5
- w_up: float32 [512, 2048], P('dp', 'tensor'), may hold values from -0.25 to 0.25
- w_down_t: float32 [512, 2048], P('dp', 'tensor'), may hold values from -0.125 to 0.125
- w_time: float32 [512, 512], replicated, may hold values from -0.25 to 0.25
- b_time: float32 [512], replicated, may hold values from -3 to 3
- ln1_gain: float32 [512], replicated, may hold values from 0.1 to 1.9
- ln1_bias: float32 [512], replicated, may hold values from -3 to 3
- ln2_gain: float32 [512], replicated, may hold values from 0.1 to 1.9
- ln2_bias: float32 [512], replicated, may hold values from -3 to 3
- b_up: float32 [2048], replicated, may hold values from -3 to 3
- b_down: float32 [512], replicated, may hold values from -3 to 3
- cotangent: bfloat16 [32, 1024, 512], P(('dp', 'tensor')), may hold values from -6 to 6
Outputs:
- layer_out: bfloat16 [32, 1024, 512], P(('dp', 'tensor'))
- grad_tokens: float32 [32, 1024, 512], P(('dp', 'tensor'))
- grad_w_qkv: float32 [3, 512, 512], P(None, 'dp', 'tensor')
- grad_w_out_t: float32 [512, 512], P('dp', 'tensor')
- grad_w_up: float32 [512, 2048], P('dp', 'tensor')
- grad_w_down_t: float32 [512, 2048], P('dp', 'tensor')
- grad_w_time: float32 [512, 512], replicated
- grad_b_time: float32 [512], replicated
- grad_ln1_gain: float32 [512], replicated
- grad_ln1_bias: float32 [512], replicated
- grad_ln2_gain: float32 [512], replicated
- grad_ln2_bias: float32 [512], replicated
- grad_b_up: float32 [2048], replicated
- grad_b_down: float32 [512], replicated
Inputs may be any that keep to these rules, and one draw needn't show every extreme that they name: `segment_ids`: never falls along a row; each document has 1 to 512 positions and one has exactly that many.
All inputs are finite; a program needn't handle non-finite values.
Results may differ from a plain program's by a relative error of at most 0.013.
Values may be sent and summed in bfloat16 or wider, within the bound.
A program may use at most 192 MiB of HBM per device.

v0:
```python
import math
import jax
import jax.numpy as jnp
from jax import lax
from jax.sharding import PartitionSpec as P

HS = 64
FF = 2048
highest = lax.Precision.HIGHEST
epsilon = 1e-05
masked_score = -1e30


def split_up(value, dim, count):
    before, after = (value.shape[:dim], value.shape[dim + 1 :])
    return jnp.moveaxis(value.reshape(*before, count, -1, *after), dim, 0)


def sent_and_summed(value, axis, dim):
    count = lax.axis_size(axis)
    parts = lax.all_to_all(split_up(value, dim, count), axis, 0, 0, tiled=True)
    return jnp.sum(parts.astype(jnp.float32), axis=0)


def side_by_side(arrays, axis, dim, along):
    ends, at = ([], 0)
    for a in arrays[:-1]:
        at += a.shape[along]
        ends.append(at)
    both = jnp.concatenate(arrays, axis=along)
    return tuple(jnp.split(sent_and_summed(both, axis, dim), ends, axis=along))


def norm_layer(values, gain_vec, shift_vec):
    row_mean = jnp.mean(values, axis=-1, keepdims=True)
    centred = values - row_mean
    variance = jnp.mean(centred * centred, axis=-1, keepdims=True)
    return centred * lax.rsqrt(variance + epsilon) * gain_vec + shift_vec


def time_features(timestep, features):
    half_width = features // 2
    frequency = jnp.exp(-math.log(10000.0) * jnp.arange(half_width, dtype=jnp.float32) / half_width)
    angles = timestep.astype(jnp.float32)[:, None] * frequency[None, :]
    return jnp.concatenate([jnp.sin(angles), jnp.cos(angles)], axis=1)


def allowed_keys(segment, length):
    places = jnp.arange(segment.shape[0], dtype=jnp.int32)
    same_doc = segment[:, None] == segment[None, :]
    is_valid = (places < length)[None, :] | (places[:, None] == places[None, :])
    return same_doc & is_valid


def gelu_tanh(values):
    return jax.nn.gelu(values, approximate=True)


def split_heads(values):
    return values.reshape(values.shape[0], values.shape[1] // HS, HS)


def head_scores(query_heads, key_heads, allowed):
    scores = jnp.einsum(
        "qhe,khe->hqk", query_heads, key_heads, preferred_element_type=jnp.float32
    ) * (1.0 / math.sqrt(HS))
    return jnp.where(allowed[None], scores, masked_score)


def attend_forward(packed):
    query_heads = split_heads(packed[0])
    key_heads = split_heads(packed[1])
    value_heads = split_heads(packed[2])
    scores = head_scores(query_heads, key_heads, allowed_keys(packed[3], packed[4]))
    row_max = jnp.max(scores, axis=-1, keepdims=True)
    raised = jnp.exp(scores - row_max)
    row_total = jnp.sum(raised, axis=-1, keepdims=True)
    probs_low = (raised / row_total).astype(jnp.bfloat16)
    mixed = jnp.einsum("hqk,khe->qhe", probs_low, value_heads, preferred_element_type=jnp.float32)
    return (mixed.reshape(packed[0].shape).astype(jnp.bfloat16), row_max + jnp.log(row_total))


def attend_backward(packed):
    query_heads = split_heads(packed[0])
    key_heads = split_heads(packed[1])
    value_heads = split_heads(packed[2])
    grad_heads = split_heads(packed[3])
    scores = head_scores(query_heads, key_heads, allowed_keys(packed[5], packed[6]))
    attn_probs = jnp.exp(scores - packed[4])
    probs_low = attn_probs.astype(jnp.bfloat16)
    grad_values = jnp.einsum(
        "hqk,qhe->khe", probs_low, grad_heads, preferred_element_type=jnp.float32
    )
    grad_probs = jnp.einsum(
        "qhe,khe->hqk", grad_heads, value_heads, preferred_element_type=jnp.float32
    )
    row_delta = jnp.sum(attn_probs * grad_probs, axis=-1, keepdims=True)
    grad_scores = (attn_probs * (grad_probs - row_delta)).astype(jnp.bfloat16)
    score_scale = 1.0 / math.sqrt(HS)
    grad_queries = (
        jnp.einsum("hqk,khe->qhe", grad_scores, key_heads, preferred_element_type=jnp.float32)
        * score_scale
    )
    grad_keys = (
        jnp.einsum("hqk,qhe->khe", grad_scores, query_heads, preferred_element_type=jnp.float32)
        * score_scale
    )
    shape_rows = packed[0].shape
    return jnp.stack(
        [
            grad_queries.reshape(shape_rows),
            grad_keys.reshape(shape_rows),
            grad_values.reshape(shape_rows),
        ]
    ).astype(jnp.bfloat16)


def shards(
    tokens,
    timestep,
    segment_ids,
    span_lengths,
    w_qkv,
    w_out_t,
    w_up,
    w_down_t,
    w_time,
    b_time,
    ln1_gain,
    ln1_bias,
    ln2_gain,
    ln2_bias,
    b_up,
    b_down,
    cotangent,
):

    def whole(w, dim):
        w = lax.all_gather(w.astype(jnp.bfloat16), "tensor", axis=dim + 1, tiled=True)
        return lax.all_gather(w, "dp", axis=dim, tiled=True)

    def part(g, dim):
        g = lax.psum_scatter(g.astype(jnp.bfloat16), "dp", scatter_dimension=dim, tiled=True)
        return lax.psum_scatter(g, "tensor", scatter_dimension=dim + 1, tiled=True).astype(
            jnp.float32
        )

    qkv_copy, out_copy, up_copy, down_copy = (
        whole(w_qkv, 1),
        whole(w_out_t, 0),
        whole(w_up, 0),
        whole(w_down_t, 0),
    )
    row = lax.axis_index("tensor")
    rows = tokens.shape[0]
    own_ids = lax.dynamic_slice_in_dim(segment_ids, row * rows, rows, 0)
    own_len = lax.dynamic_slice_in_dim(span_lengths, row * rows, rows, 0)
    time_emb = time_features(timestep, tokens.shape[2])
    time_proj = jnp.dot(time_emb, w_time, precision=highest) + b_time
    start = tokens.astype(jnp.float32) + time_proj[:, None, :]
    normed_one = norm_layer(start, ln1_gain, ln1_bias).astype(jnp.bfloat16)
    qkv_act = jnp.einsum(
        "nsd,cde->cnse", normed_one, qkv_copy, preferred_element_type=jnp.float32
    ).astype(jnp.bfloat16)
    mixed, log_total = lax.map(
        attend_forward, (qkv_act[0], qkv_act[1], qkv_act[2], own_ids, own_len)
    )
    attn_out = jnp.einsum("nse,de->nsd", mixed, out_copy, preferred_element_type=jnp.float32)
    middle = start + attn_out
    normed_two = norm_layer(middle, ln2_gain, ln2_bias).astype(jnp.bfloat16)
    upper = (
        jnp.einsum("nsd,df->nsf", normed_two, up_copy, preferred_element_type=jnp.float32) + b_up
    )
    activated = gelu_tanh(upper).astype(jnp.bfloat16)
    ffn_out = jnp.einsum("nsf,df->nsd", activated, down_copy, preferred_element_type=jnp.float32)
    layer_out = (middle + ffn_out + b_down).astype(jnp.bfloat16)
    grad_b_down = jnp.sum(cotangent.astype(jnp.float32), axis=(0, 1))
    grad_down = jnp.einsum("nsd,nsf->df", cotangent, activated, preferred_element_type=jnp.float32)
    grad_act = jnp.einsum("nsd,df->nsf", cotangent, down_copy, preferred_element_type=jnp.float32)
    gelu_value, gelu_pull = jax.vjp(gelu_tanh, upper)
    grad_upper = gelu_pull(grad_act)[0].astype(jnp.bfloat16)
    grad_bias_up = jnp.sum(grad_upper.astype(jnp.float32), axis=(0, 1))
    grad_up = jnp.einsum("nsd,nsf->df", normed_two, grad_upper, preferred_element_type=jnp.float32)
    grad_normed_two = jnp.einsum(
        "nsf,df->nsd", grad_upper, up_copy, preferred_element_type=jnp.float32
    )
    norm_two_value, norm_two_pull = jax.vjp(norm_layer, middle, ln2_gain, ln2_bias)
    grad_middle_norm, grad_gain_two, grad_bias_two = norm_two_pull(grad_normed_two)
    grad_middle = cotangent.astype(jnp.float32) + grad_middle_norm
    grad_attn = grad_middle.astype(jnp.bfloat16)
    grad_out_w = jnp.einsum("nsd,nse->de", grad_attn, mixed, preferred_element_type=jnp.float32)
    grad_mixed = jnp.einsum(
        "nsd,de->nse", grad_attn, out_copy, preferred_element_type=jnp.float32
    ).astype(jnp.bfloat16)
    grad_qkv_act = lax.map(
        attend_backward,
        (qkv_act[0], qkv_act[1], qkv_act[2], grad_mixed, log_total, own_ids, own_len),
    )
    grad_qkv_w = jnp.einsum(
        "nsd,ncse->cde", normed_one, grad_qkv_act, preferred_element_type=jnp.float32
    )
    grad_normed_one = jnp.einsum(
        "ncse,cde->nsd", grad_qkv_act, qkv_copy, preferred_element_type=jnp.float32
    )
    norm_one_value, norm_one_pull = jax.vjp(norm_layer, start, ln1_gain, ln1_bias)
    grad_start_norm, grad_gain_one, grad_bias_one = norm_one_pull(grad_normed_one)
    grad_tokens = grad_middle + grad_start_norm
    grad_time_rows = jnp.sum(grad_tokens, axis=1)
    lines = jnp.concatenate([time_emb, grad_time_rows], axis=1)
    lines = lax.all_gather(lines, ("dp", "tensor"), axis=0, tiled=True)
    all_emb, all_grad = (lines[:, : time_emb.shape[1]], lines[:, time_emb.shape[1] :])
    grad_time_w = jnp.dot(all_emb.T, all_grad, precision=highest)
    grad_time_bias = jnp.sum(all_grad, axis=0)
    small = jnp.concatenate(
        [grad_gain_one, grad_bias_one, grad_gain_two, grad_bias_two, grad_b_down, grad_bias_up]
    )
    small = lax.psum(small, ("dp", "tensor"))
    cuts = jnp.split(small, [tokens.shape[2] * k for k in range(1, 6)])
    return (
        layer_out,
        grad_tokens,
        part(grad_qkv_w, 1),
        part(grad_out_w, 0),
        part(grad_up, 0),
        part(grad_down, 0),
        grad_time_w,
        grad_time_bias,
        cuts[0],
        cuts[1],
        cuts[2],
        cuts[3],
        cuts[5],
        cuts[4],
    )


def solution(mesh):
    return jax.shard_map(
        shards,
        mesh=mesh,
        in_specs=(
            P(("dp", "tensor"), None, None),
            P(("dp", "tensor")),
            P("dp", None),
            P("dp"),
            P(None, "dp", "tensor"),
            P("dp", "tensor"),
            P("dp", "tensor"),
            P("dp", "tensor"),
            P(),
            P(),
            P(),
            P(),
            P(),
            P(),
            P(),
            P(),
            P(("dp", "tensor"), None, None),
        ),
        out_specs=(
            P(("dp", "tensor"), None, None),
            P(("dp", "tensor"), None, None),
            P(None, "dp", "tensor"),
            P("dp", "tensor"),
            P("dp", "tensor"),
            P("dp", "tensor"),
            P(),
            P(),
            P(),
            P(),
            P(),
            P(),
            P(),
            P(),
        ),
        check_vma=False,
    )
```

profile of v0, /device:TPU:0, one launch (start us, length us, event | category | flops | bytes accessed | tf_op | source)
XLA Modules:
  0.0 517.9 jit_solution(3765666602704823875)
XLA Ops:
  8.3 14.8 %all_gather.27 = bf16[3,64,512]{2,1,0:T(8,128)(2,1)} all-gather(bf16[3,64,128]{2,1,0:T(8,128)(2,1)S(1)} %convert_element_type.127), channel_id=1, replica_groups=mesh['dp'=8,'tensor'=4] {'tensor'}, dimensions={2}, use_global_device_ids=true | all-gather | bytes 245760 | tf_op jit(solution)/shard_map/all_gather | solution.py:139
  24.1 15.1 %all_gather.31 = bf16[64,2048]{1,0:T(8,128)(2,1)} all-gather(bf16[64,512]{1,0:T(8,128)(2,1)S(1)} %convert_element_type.138), channel_id=1, replica_groups=mesh['dp'=8,'tensor'=4] {'tensor'}, dimensions={1}, use_global_device_ids=true | all-gather | bytes 327680 | tf_op jit(solution)/shard_map/all_gather | solution.py:139
  40.2 14.9 %all_gather.33 = bf16[64,2048]{1,0:T(8,128)(2,1)} all-gather(bf16[64,512]{1,0:T(8,128)(2,1)S(1)} %convert_element_type.140), channel_id=1, replica_groups=mesh['dp'=8,'tensor'=4] {'tensor'}, dimensions={1}, use_global_device_ids=true | all-gather | bytes 327680 | tf_op jit(solution)/shard_map/all_gather | solution.py:139
  58.0 12.0 %all_gather.29 = bf16[64,512]{1,0:T(8,128)(2,1)S(1)} all-gather(bf16[64,128]{1,0:T(8,128)(2,1)S(1)} %convert_element_type.136), channel_id=1, replica_groups=mesh['dp'=8,'tensor'=4] {'tensor'}, dimensions={1}, use_global_device_ids=true | all-gather | bytes 81920 | tf_op jit(solution)/shard_map/all_gather | solution.py:139
  69.9 11.6 %all_gather.30 = bf16[512,512]{1,0:T(8,128)(2,1)} all-gather(bf16[64,512]{1,0:T(8,128)(2,1)S(1)} %all_gather.29), channel_id=1, replica_groups=mesh['dp'=8,'tensor'=4] {'dp'}, dimensions={0}, use_global_device_ids=true | all-gather | bytes 589824 | tf_op jit(solution)/shard_map/all_gather | solution.py:140
  84.5 2.3 fusion.14
  86.8 3.5 convert_bitcast_fusion
  91.7 14.0 %fusion.59 = (f32[8,1024]{1,0:T(8,128)S(1)}, f32[8,1024,1024]{1,2,0:T(8,128)}) fusion(bf16[1024,8,64]{0,2,1:T(8,128)(2,1)S(1)} %bitcast.135, bf16[1024,8,64]{0,2,1:T(8,128)(2,1)S(1)} %bitcast.133, pred[1024,1024]{0,1:T(8,128)(4,1)S(1)} %copy-done.15), kind=kOutput, calls=%fused_computation.112 | convolution fusion | flops 1098899456 | bytes 36732928 | tf_op jit(solution)/shard_map/while/body/eval_jaxpr/qhe,khe->hqk/dot_general | solution.py:64
  105.7 13.1 %fusion = f32[8,1024]{1,0:T(8,128)S(1)} fusion(f32[8,1024,1024]{1,2,0:T(8,128)} %get-tuple-element.125, f32[8,1024]{1,0:T(8,128)S(1)} %get-tuple-element.124), kind=kLoop, calls=%fused_computation.6 | loop fusion | flops 16769024 | bytes 33619968 | tf_op jit(solution)/shard_map/while/body/eval_jaxpr/reduce_sum | solution.py:77
  118.8 14.0 %fusion.29 = bf16[8,64,1024]{2,1,0:T(8,128)(2,1)S(1)} fusion(bf16[1024,8,64]{0,2,1:T(8,128)(2,1)S(1)} %bitcast.140, f32[8,1024,1024]{1,2,0:T(8,128)} %get-tuple-element.125, f32[8,1024]{1,0:T(8,128)S(1)} %fusion, f32[8,1024]{1,0:T(8,128)S(1)} %get-tuple-element.124), kind=kOutput, calls=%fused_computation.62 | convolution fusion | flops 1099431936 | bytes 35717120 | tf_op jit(solution)/shard_map/while/body/eval_jaxpr/hqk,khe->qhe/dot_general | solution.py:79
  135.6 11.5 %multiply_convert_fusion.1 = (bf16[1024,2048]{1,0:T(8,128)(2,1)}, f32[1024,2048]{1,0:T(8,128)}) fusion(f32[2048]{0:T(1024)S(1)} %copy-done.46, bf16[512,2048]{1,0:T(8,128)(2,1)} %all-gather.7.cloned.1.call-done, f32[1,1024,512]{1,2,0:T(8,128)} %copy-done.5, f32[512]{0:T(512)S(1)} %copy-done.49, f32[512]{0:T(512)S(1)} %copy-done.43, f32[1024]{0:T(1024)S(1)} %fusion.40, ...), kind=kOutput, calls=%fused_computation.21 | convolution fusion | flops 2171076608 | bytes 16797696 | tf_op jit(solution)/shard_map/nsd,df->nsf/dot_general | solution.py:172
  147.1 10.2 %convert_reduce_fusion = (f32[2048]{0:T(1024)S(1)}, bf16[1024,2048]{1,0:T(8,128)(2,1)S(1)}) fusion(f32[1024,2048]{1,0:T(8,128)} %get-tuple-element.129, f32[2048]{0:T(1024)S(1)} %copy-done.46, bf16[512,2048]{1,0:T(8,128)(2,1)} %all-gather.9.cloned.1.call-done, bf16[1,1024,512]{2,1,0:T(8,128)(2,1)S(1)} %copy-done.24), kind=kOutput, calls=%fused_computation.20 | convolution fusion | flops 2195716096 | bytes 15745024 | tf_op jit(solution)/shard_map/nsd,df->nsf/dot_general | solution.py:179
  157.3 3.7 fusion.62
  161.0 3.0 copy.79
  164.0 3.0 fusion.16
  170.0 1.6 convolution_convert_fusion.4
  171.6 2.0 convolution_convert_fusion.3
  173.6 14.4 %fusion.25 = bf16[8,64,1024]{2,1,0:T(8,128)(2,1)} fusion(bf16[1024,8,64]{0,2,1:T(8,128)(2,1)S(1)} %bitcast.138, f32[8,1024,1024]{1,2,0:T(8,128)} %get-tuple-element.125, f32[8,1024]{1,0:T(8,128)S(1)} %log_add_fusion), kind=kOutput, calls=%fused_computation.59 | convolution fusion | flops 1091043328 | bytes 35684352 | tf_op jit(solution)/shard_map/while/body/eval_jaxpr/hqk,qhe->khe/dot_general | solution.py:91
  188.0 22.0 %multiply_reduce_fusion = (f32[8,1024]{1,0:T(8,128)S(1)}, f32[8,1024,1024]{1,2,0:T(8,128)}) fusion(f32[8,1024,1024]{1,2,0:T(8,128)} %get-tuple-element.125, f32[8,1024]{1,0:T(8,128)S(1)} %log_add_fusion, bf16[1024,8,64]{0,2,1:T(8,128)(2,1)S(1)} %bitcast.139, bf16[1024,8,64]{0,2,1:T(8,128)(2,1)S(1)} %bitcast.141), kind=kOutput, calls=%fused_computation.1 | convolution fusion | flops 1098899456 | bytes 69271552 | tf_op jit(solution)/shard_map/while/body/eval_jaxpr/qhe,khe->hqk/dot_general | solution.py:94
  210.1 28.7 %multiply_convert_fusion = bf16[8,1024,1024]{1,2,0:T(8,128)(2,1)} fusion(f32[8,1024,1024]{1,2,0:T(8,128)} %get-tuple-element.131, f32[8,1024,1024]{1,2,0:T(8,128)} %get-tuple-element.125, f32[8,1024]{1,0:T(8,128)S(1)} %get-tuple-element.130, f32[8,1024]{1,0:T(8,128)S(1)} %log_add_fusion), kind=kLoop, calls=%fused_computation | loop fusion | flops 33554432 | bytes 83951616 | tf_op jit(solution)/shard_map/while/body/eval_jaxpr/convert_element_type | solution.py:98
  238.9 12.1 %multiply_convert_fusion.2 = bf16[8,64,1024]{2,1,0:T(8,128)(2,1)} fusion(bf16[1024,8,64]{0,2,1:T(8,128)(2,1)S(1)} %bitcast.136, bf16[8,1024,1024]{1,2,0:T(8,128)(2,1)} %multiply_convert_fusion), kind=kOutput, calls=%fused_computation.47 | convolution fusion | flops 1074790400 | bytes 18874368 | tf_op jit(solution)/shard_map/while/body/eval_jaxpr/hqk,qhe->khe/dot_general | solution.py:105
  250.9 9.9 %multiply_convert_fusion.3 = bf16[8,64,1024]{2,1,0:T(8,128)(2,1)} fusion(bf16[1024,8,64]{0,2,1:T(8,128)(2,1)S(1)} %bitcast.134, bf16[8,1024,1024]{1,2,0:T(8,128)(2,1)} %multiply_convert_fusion), kind=kOutput, calls=%fused_computation.48 | convolution fusion | flops 1074790400 | bytes 18874368 | tf_op jit(solution)/shard_map/while/body/eval_jaxpr/hqk,khe->qhe/dot_general | solution.py:101
  262.1 2.4 copy.83
  265.9 4.8 fusion.28
  270.7 4.4 copy.89
  275.2 6.7 %convolution_convert_fusion.1 = bf16[512,2048]{1,0:T(8,128)(2,1)} fusion(bf16[1024,2048]{1,0:T(8,128)(2,1)} %copy-done.55, f32[1,1024,512]{1,2,0:T(8,128)} %copy-done.5, f32[512]{0:T(512)S(1)} %copy-done.49, f32[512]{0:T(512)S(1)} %copy-done.43, f32[1024]{0:T(1024)S(1)} %fusion.40, f32[1024]{0:T(1024)S(1)} %broadcast_multiply_fusion), kind=kOutput, calls=%fused_computation.30 | convolution fusion | flops 2151153664 | bytes 8400896 | tf_op jit(solution)/shard_map/nsd,nsf->df/dot_general | solution.py:183
  283.1 6.0 %fusion.15 = bf16[512,2048]{0,1:T(8,128)(2,1)} fusion(bf16[1024,2048]{1,0:T(8,128)(2,1)} %get-tuple-element.128, bf16[1,1024,512]{2,1,0:T(8,128)(2,1)S(1)} %copy-done.25), kind=kOutput, calls=%fused_computation.31 | convolution fusion | flops 2148532224 | bytes 7340032 | tf_op jit(solution)/shard_map/nsd,nsf->df/dot_general | solution.py:178
  289.1 4.0 copy.110
  295.0 4.9 fusion.61
  299.9 2.9 copy.86
  302.8 2.3 fusion.18
  306.9 2.6 fusion.55
  309.6 1.6 copy.108
  311.3 24.4 %all-reduce.3.cloned.1.call-done = bf16[3,512,512]{2,0,1:T(4,128)(2,1)} async-done(((bf16[3,512,512]{2,0,1:T(4,128)(2,1)}), bf16[3,512,512]{2,0,1:T(4,128)(2,1)}) %all-reduce.3.cloned.1.call-update) | async-done | bytes 1572880
  336.7 14.0 %copy.106 = bf16[3,64,512]{0,1,2:T(8,128)(2,1)} copy(bf16[3,64,512]{2,0,1:T(4,128)(2,1)S(1)} %constant_dynamic-slice_fusion) | data formatting | bytes 393216
  350.7 13.9 %reshape.435 = bf16[512,192]{1,0:T(8,128)(2,1)} reshape(bf16[512,64,3]{2,1,0:T(8,128)(2,1)} %bitcast.132) | data formatting | bytes 393216
  364.6 67.5 %all-gather = f32[32,1,1024]{2,1,0:T(1,128)S(1)} all-gather(f32[1,1,1024]{2,1,0:T(1,128)S(1)} %maximum_bitcast_fusion), channel_id=1, replica_groups=mesh['dp'=8,'tensor'=4] {'dp','tensor'}, dimensions={0}, use_global_device_ids=true | all-gather | bytes 135168 | tf_op jit(solution)/shard_map/all_gather | solution.py:210
  433.2 5.2 %fusion.21 = bf16[1,1024,512]{1,2,0:T(8,128)(2,1)S(1)} fusion(f32[1,1024,512]{1,2,0:T(8,128)S(1)} %copy-done.7, bf16[1024,2048]{1,0:T(8,128)(2,1)} %get-tuple-element.128, bf16[512,2048]{1,0:T(8,128)(2,1)} %all-gather.9.cloned.1.call-done, f32[512]{0:T(512)S(1)} %copy-done.50), kind=kOutput, calls=%fused_computation.44 | convolution fusion | flops 2149056512 | bytes 9439232 | tf_op jit(solution)/shard_map/nsf,df->nsd/dot_general | solution.py:175
  438.5 2.1 copy.111
  440.6 1.3 copy.92
  441.9 37.5 %psum.7 = f32[4608]{0:T(1024)S(1)} all-reduce(f32[4608]{0:T(1024)S(1)} %constant_dynamic-update-slice_fusion), channel_id=1, replica_groups=mesh['dp'=8,'tensor'=4] {'dp','tensor'}, use_global_device_ids=true, to_apply=%region_27.28 | all-reduce | flops 4608 | bytes 36864 | tf_op jit(solution)/shard_map/psum | solution.py:217
  480.0 1.8 copy.93
  482.4 2.0 fusion.36
  485.9 5.3 %reshape.436 = bf16[128,64,3]{2,1,0:T(8,128)(2,1)S(1)} reshape(bf16[128,192]{1,0:T(8,128)(2,1)} %reduce-scatter.22.cloned.1.call-done) | data formatting | bytes 98304
  491.2 2.2 copy.107
  494.1 1.5 convert_element_type.154
  495.6 13.7 %reduce-scatter.20.cloned.1.call-done = bf16[64,512]{0,1:T(8,128)(2,1)} async-done(((bf16[64,2048]{0,1:T(8,128)(2,1)}), bf16[64,512]{0,1:T(8,128)(2,1)}) %reduce-scatter.20.cloned.1.call-update) | async-done | bytes 65552 | tf_op jit(solution)/shard_map/reduce_scatter | solution.py:144
  509.3 1.6 copy.95
  (191 shorter events, 27.4 us)
Async XLA Ops:
  7.2 74.9 %copy-start = (f32[512,512]{1,0:T(8,128)S(1)}, f32[512,512]{1,0:T(8,128)}, u32[]{:S(2)}) copy-start(f32[512,512]{1,0:T(8,128)} %param.25) | copy-start | bytes 3145732
  7.2 48.7 %copy-start.51 = (s32[4]{0:T(128)S(1)}, s32[4]{0:T(128)}, u32[]{:S(2)}) copy-start(s32[4]{0:T(128)} %param.20) | copy-start | bytes 52
  7.2 50.7 %copy-start.36 = (f32[64,128]{1,0:T(8,128)S(1)}, f32[64,128]{1,0:T(8,128)}, u32[]{:S(2)}) copy-start(f32[64,128]{1,0:T(8,128)} %param.22) | copy-start | bytes 98308
  7.2 74.4 %copy-start.22 = (bf16[1,1024,512]{2,1,0:T(8,128)(2,1)S(1)}, bf16[1,1024,512]{2,1,0:T(8,128)(2,1)}, u32[]{:S(2)}) copy-start(bf16[1,1024,512]{2,1,0:T(8,128)(2,1)} %param.17) | copy-start | bytes 3145732
  7.2 79.6 %all-gather.5.cloned.1.call-start = ((), (), s32[]{:S(2)}) async-start(), calls=%async_computation.7 | async-start | bytes 1769472 | tf_op jit(solution)/shard_map/all_gather | solution.py:140
  23.1 112.4 %all-gather.7.cloned.1.call-start = ((), (), s32[]{:S(2)}) async-start(), calls=%async_computation.8 | async-start | bytes 2359296 | tf_op jit(solution)/shard_map/all_gather | solution.py:140
  39.2 107.9 %all-gather.9.cloned.1.call-start = ((), (), s32[]{:S(2)}) async-start(), calls=%async_computation.9 | async-start | bytes 2359296 | tf_op jit(solution)/shard_map/all_gather | solution.py:140
  55.1 27.6 %copy-start.44 = (f32[512]{0:T(512)S(1)}, f32[512]{0:T(512)}, u32[]{:S(2)}) copy-start(f32[512]{0:T(512)} %param.26) | copy-start | bytes 6148
  55.2 254.4 %reduce-scatter.14.cloned.1.call-start = ((), (), s32[]{:S(2)}) async-start(), calls=%async_computation.10 | async-start | bytes 589824 | tf_op jit(solution)/shard_map/reduce_scatter | solution.py:143
  57.2 25.6 %copy-start.41 = (f32[1,256]{1,0:T(1,128)}, f32[1,256]{1,0:T(1,128)S(1)}, u32[]{:S(2)}) copy-start(f32[1,256]{1,0:T(1,128)S(1)} %get-tuple-element.139) | copy-start | bytes 3076
  57.2 25.6 %copy-start.39 = (f32[1,256]{1,0:T(1,128)}, f32[1,256]{1,0:T(1,128)S(1)}, u32[]{:S(2)}) copy-start(f32[1,256]{1,0:T(1,128)S(1)} %get-tuple-element.138) | copy-start | bytes 3076
  83.1 3.7 copy-start.30
  83.1 3.7 copy-start.37
  83.1 3.7 copy-start.47
  83.5 6.8 %copy-start.34 = (f32[1024]{0:T(1024)}, f32[1024]{0:T(1024)S(1)}, u32[]{:S(2)}) copy-start(f32[1024]{0:T(1024)S(1)} %multiply_reduce_fusion.2) | copy-start | bytes 12292
  84.0 6.3 %copy-start.32 = (f32[1024]{0:T(1024)}, f32[1024]{0:T(1024)S(1)}, u32[]{:S(2)}) copy-start(f32[1024]{0:T(1024)S(1)} %fusion.39) | copy-start | bytes 12292
  84.5 83.5 %copy-start.13 = (bf16[1,1024,512]{1,2,0:T(8,128)(2,1)}, bf16[1,1024,512]{1,2,0:T(8,128)(2,1)S(1)}, u32[]{:S(2)}) copy-start(bf16[1,1024,512]{1,2,0:T(8,128)(2,1)S(1)} %copy.78) | copy-start | bytes 3145732
  90.6 15.0 %copy-start.9 = (bf16[1,1,1024,512]{2,3,0,1:T(8,128)(2,1)}, bf16[1,1,1024,512]{2,3,0,1:T(8,128)(2,1)S(1)}, u32[]{:S(2)}) copy-start(bf16[1,1,1024,512]{2,3,0,1:T(8,128)(2,1)S(1)} %get-tuple-element.115) | copy-start | bytes 3145732
  90.7 15.0 %copy-start.11 = (bf16[1,1,1024,512]{2,3,0,1:T(8,128)(2,1)}, bf16[1,1,1024,512]{2,3,0,1:T(8,128)(2,1)S(1)}, u32[]{:S(2)}) copy-start(bf16[1,1,1024,512]{2,3,0,1:T(8,128)(2,1)S(1)} %get-tuple-element.116) | copy-start | bytes 3145732
  90.7 28.1 %copy-start.17 = (bf16[1,1,1024,512]{2,3,0,1:T(8,128)(2,1)}, bf16[1,1,1024,512]{2,3,0,1:T(8,128)(2,1)S(1)}, u32[]{:S(2)}) copy-start(bf16[1,1,1024,512]{2,3,0,1:T(8,128)(2,1)S(1)} %get-tuple-element.117) | copy-start | bytes 3145732
  118.8 14.1 %copy-start.28 = (bf16[512,512]{1,0:T(8,128)(2,1)S(1)}, bf16[512,512]{1,0:T(8,128)(2,1)}, u32[]{:S(2)}) copy-start(bf16[512,512]{1,0:T(8,128)(2,1)} %all_gather.30) | copy-start | bytes 1572868
  135.5 11.6 %copy-start.24 = (bf16[1,1024,512]{2,1,0:T(8,128)(2,1)S(1)}, bf16[1,1024,512]{2,1,0:T(8,128)(2,1)}, u32[]{:S(2)}) copy-start(bf16[1,1024,512]{2,1,0:T(8,128)(2,1)} %param.33) | copy-start | bytes 3145732
  147.1 10.3 %copy-start.45 = (bf16[512,2048]{1,0:T(8,128)(2,1)S(1)}, bf16[512,2048]{1,0:T(8,128)(2,1)}, u32[]{:S(2)}) copy-start(bf16[512,2048]{1,0:T(8,128)(2,1)} %all-gather.7.cloned.1.call-done) | copy-start | bytes 6291460
  157.3 3.7 copy-start.55
  164.0 3.0 copy-start.6
  164.0 3.5 copy-start.8
  173.6 14.4 %copy-start.18 = (bf16[1,1,1024,512]{2,3,0,1:T(8,128)(2,1)S(1)}, bf16[1,1,1024,512]{2,3,0,1:T(8,128)(2,1)}, u32[]{:S(2)}) copy-start(bf16[1,1,1024,512]{2,3,0,1:T(8,128)(2,1)} %copy-done.17) | copy-start | bytes 3145732
  210.1 125.6 %all-reduce.3.cloned.1.call-start = ((), (), s32[]{:S(2)}) async-start(), calls=%async_computation.17 | async-start | bytes 4194304
  210.1 28.7 %copy-start.12 = (bf16[1,1,1024,512]{2,3,0,1:T(8,128)(2,1)S(1)}, bf16[1,1,1024,512]{2,3,0,1:T(8,128)(2,1)}, u32[]{:S(2)}) copy-start(bf16[1,1,1024,512]{2,3,0,1:T(8,128)(2,1)} %copy-done.11) | copy-start | bytes 3145732
  238.9 12.1 %copy-start.10 = (bf16[1,1,1024,512]{2,3,0,1:T(8,128)(2,1)S(1)}, bf16[1,1,1024,512]{2,3,0,1:T(8,128)(2,1)}, u32[]{:S(2)}) copy-start(bf16[1,1,1024,512]{2,3,0,1:T(8,128)(2,1)} %copy-done.9) | copy-start | bytes 3145732
  250.9 9.9 %copy-start.19 = (bf16[8,64,1024]{2,1,0:T(8,128)(2,1)S(1)}, bf16[8,64,1024]{2,1,0:T(8,128)(2,1)}, u32[]{:S(2)}) copy-start(bf16[8,64,1024]{2,1,0:T(8,128)(2,1)} %fusion.25) | copy-start | bytes 3145732
  260.8 3.7 copy-start.20
  262.1 3.7 copy-start.26
  262.1 3.7 copy-start.31
  262.1 3.7 copy-start.33
  262.1 3.7 copy-start.38
  262.1 3.7 copy-start.48
  275.1 157.7 %reduce-scatter.16.cloned.1.call-start = ((), (), s32[]{:S(2)}) async-start(), calls=%async_computation.11 | async-start | bytes 2359296 | tf_op jit(solution)/shard_map/reduce_scatter | solution.py:143
  281.9 156.6 %reduce-scatter.26.cloned.1.call-start = ((), (), s32[]{:S(2)}) async-start(), calls=%async_computation.16 | async-start | bytes 2359296
  293.1 191.3 %reduce-scatter.24.cloned.1.call-start = ((), (), s32[]{:S(2)}) async-start(), calls=%async_computation.15 | async-start | bytes 163840
  306.9 2.6 copy-start.42
  311.2 174.7 %reduce-scatter.22.cloned.1.call-start = ((), (), s32[]{:S(2)}) async-start(), calls=%async_computation.14 | async-start | bytes 327680
  350.7 82.5 %copy-start.7 = (f32[1,1024,512]{1,2,0:T(8,128)S(1)}, f32[1,1024,512]{1,2,0:T(8,128)}, u32[]{:S(2)}) copy-start(f32[1,1024,512]{1,2,0:T(8,128)} %copy-done.5) | copy-start | bytes 6291460
  350.7 82.5 %copy-start.50 = (f32[512]{0:T(512)S(1)}, f32[512]{0:T(512)}, u32[]{:S(2)}) copy-start(f32[512]{0:T(512)} %param.32) | copy-start | bytes 6148
  364.6 129.5 %reduce-scatter.18.cloned.1.call-start = ((), (), s32[]{:S(2)}) async-start(), calls=%async_computation.12 | async-start | bytes 327680 | tf_op jit(solution)/shard_map/reduce_scatter | solution.py:144
  432.9 76.4 %reduce-scatter.20.cloned.1.call-start = ((), (), s32[]{:S(2)}) async-start(), calls=%async_computation.13 | async-start | bytes 655360 | tf_op jit(solution)/shard_map/reduce_scatter | solution.py:144
  438.4 41.6 %copy-start.16 = (f32[1,1024,512]{1,2,0:T(8,128)S(1)}, f32[1,1024,512]{1,2,0:T(8,128)}, u32[]{:S(2)}) copy-start(f32[1,1024,512]{1,2,0:T(8,128)} %get-tuple-element.112) | copy-start | bytes 6291460
  485.2 25.7 %copy-start.1 = (f32[512,512]{1,0:T(8,128)S(1)}, f32[512,512]{1,0:T(8,128)}, u32[]{:S(2)}) copy-start(f32[512,512]{1,0:T(8,128)} %param.25) | copy-start | bytes 3145732
  (19 other events, 30.9 us)
Sparse Core Ops, SparseCore 0:
  23.3 25.8 all-gather.4
  51.1 28.5 all-gather.6
  81.6 29.2 all-gather.8
  210.2 32.9 reduce-scatter.13
  275.3 60.3 all-reduce.2
  339.2 40.4 reduce-scatter.15
  382.9 41.2 reduce-scatter.25
  427.1 19.2 reduce-scatter.23
  448.6 18.0 reduce-scatter.21
  468.9 18.1 reduce-scatter.17
  489.4 19.8 reduce-scatter.19
where the time goes:
time: 528 us; the launch traced here: 518 us
  blocking collectives  173 us (33%)
  matrix products  150 us (28%)
  local copies, waits for them, and re-layouts  77.5 us (15%)
  other arithmetic  61.4 us (12%)
  waiting for transfers between devices  38.4 us (7%)
  between operations  16.4 us (3%)
    all_gather x1, blocking collectives, shards(): lines = lax.all_gather(lines, ('dp', 'tensor'), axis=0, tiled=True)  67.5 us
    unnamed x134, local copies, waits for them, and re-layouts  59.4 us
    all_gather x4, blocking collectives, whole(): lax.all_gather(w.astype(jnp.bfloat16), 'tensor', axis=dim + 1, tiled=True)  56.8 us
    psum x1, blocking collectives, shards(): small = lax.psum(small, ('dp', 'tensor'))  37.5 us
    convert_element_type x1, other arithmetic, attend_backward(): grad_scores = (attn_probs * (grad_probs - row_delta)).astype(jnp.bfloat16)  28.7 us
    unnamed x15, waiting for transfers between devices  24.6 us
    dot_general x1, matrix products, attend_backward(): jnp.einsum('qhe,khe->hqk', grad_heads, value_heads, preferred_element_typ...  22 us
    dot_general x1, matrix products, attend_backward(): jnp.einsum('hqk,qhe->khe', probs_low, grad_heads, preferred_element_type=...  14.4 us
  transfers between devices with their start and end apart: 11, of which 2 were waited for; matrix products, arithmetic and copies ran while one was open for 42% of the time, Pallas kernels for 0%

commit v1 on v0

--- a/solution.py
+++ b/solution.py
@@ -9,6 +9,11 @@
 highest = lax.Precision.HIGHEST
 epsilon = 1e-05
 masked_score = -1e30
+
+
+def axis_by_axis(array, first, second):
+    partial = lax.psum(array, first)
+    return lax.psum(partial, second)
 
 
 def split_up(value, dim, count):
@@ -214,7 +219,7 @@
     small = jnp.concatenate(
         [grad_gain_one, grad_bias_one, grad_gain_two, grad_bias_two, grad_b_down, grad_bias_up]
     )
-    small = lax.psum(small, ("dp", "tensor"))
+    small = axis_by_axis(small, "dp", "tensor")
     cuts = jnp.split(small, [tokens.shape[2] * k for k in range(1, 6)])
     return (
         layer_out,

time: 528 us -> 528 us (level)
    psum x1 -> x2, blocking collectives: 37.5 us -> 38.5 us  [the longest x1 22.7 us: axis_by_axis(): partial = lax.psum(array, first)]
where the time goes in v1:
time: 528 us; the launch traced here: 517 us
  blocking collectives  174 us (33%)
  matrix products  150 us (28%)
  local copies, waits for them, and re-layouts  77.5 us (15%)
  other arithmetic  61.4 us (12%)
  waiting for transfers between devices  36.8 us (7%)
  between operations  16.4 us (3%)
    all_gather x1, blocking collectives, shards(): lines = lax.all_gather(lines, ('dp', 'tensor'), axis=0, tiled=True)  67.5 us
    unnamed x134, local copies, waits for them, and re-layouts  59.4 us
    all_gather x4, blocking collectives, whole(): lax.all_gather(w.astype(jnp.bfloat16), 'tensor', axis=dim + 1, tiled=True)  56.8 us
    convert_element_type x1, other arithmetic, attend_backward(): grad_scores = (attn_probs * (grad_probs - row_delta)).astype(jnp.bfloat16)  28.7 us
    unnamed x15, waiting for transfers between devices  24.6 us
    psum x1, blocking collectives, axis_by_axis(): partial = lax.psum(array, first)  22.7 us
    dot_general x1, matrix products, attend_backward(): jnp.einsum('qhe,khe->hqk', grad_heads, value_heads, preferred_element_typ...  22 us
    psum x1, blocking collectives, axis_by_axis(): return lax.psum(partial, second)  15.8 us
  transfers between devices with their start and end apart: 11, of which 2 were waited for; matrix products, arithmetic and copies ran while one was open for 42% of the time, Pallas kernels for 0%

profile of v1, /device:TPU:0, one launch (start us, length us, event | category | flops | bytes accessed | tf_op | source)
XLA Modules:
  0.0 517.3 jit_solution(12495899421546429461)
XLA Ops:
  8.3 14.8 %all_gather.27 = bf16[3,64,512]{2,1,0:T(8,128)(2,1)} all-gather(bf16[3,64,128]{2,1,0:T(8,128)(2,1)S(1)} %convert_element_type.127), channel_id=1, replica_groups=mesh['dp'=8,'tensor'=4] {'tensor'}, dimensions={2}, use_global_device_ids=true | all-gather | bytes 245760 | tf_op jit(solution)/shard_map/all_gather | solution.py:144
  24.1 15.1 %all_gather.31 = bf16[64,2048]{1,0:T(8,128)(2,1)} all-gather(bf16[64,512]{1,0:T(8,128)(2,1)S(1)} %convert_element_type.138), channel_id=1, replica_groups=mesh['dp'=8,'tensor'=4] {'tensor'}, dimensions={1}, use_global_device_ids=true | all-gather | bytes 327680 | tf_op jit(solution)/shard_map/all_gather | solution.py:144
  40.2 14.9 %all_gather.33 = bf16[64,2048]{1,0:T(8,128)(2,1)} all-gather(bf16[64,512]{1,0:T(8,128)(2,1)S(1)} %convert_element_type.140), channel_id=1, replica_groups=mesh['dp'=8,'tensor'=4] {'tensor'}, dimensions={1}, use_global_device_ids=true | all-gather | bytes 327680 | tf_op jit(solution)/shard_map/all_gather | solution.py:144
  58.0 12.0 %all_gather.29 = bf16[64,512]{1,0:T(8,128)(2,1)S(1)} all-gather(bf16[64,128]{1,0:T(8,128)(2,1)S(1)} %convert_element_type.136), channel_id=1, replica_groups=mesh['dp'=8,'tensor'=4] {'tensor'}, dimensions={1}, use_global_device_ids=true | all-gather | bytes 81920 | tf_op jit(solution)/shard_map/all_gather | solution.py:144
  69.9 11.6 %all_gather.30 = bf16[512,512]{1,0:T(8,128)(2,1)} all-gather(bf16[64,512]{1,0:T(8,128)(2,1)S(1)} %all_gather.29), channel_id=1, replica_groups=mesh['dp'=8,'tensor'=4] {'dp'}, dimensions={0}, use_global_device_ids=true | all-gather | bytes 589824 | tf_op jit(solution)/shard_map/all_gather | solution.py:145
  84.5 2.3 fusion.14
  86.8 3.5 convert_bitcast_fusion
  91.7 14.0 %fusion.59 = (f32[8,1024]{1,0:T(8,128)S(1)}, f32[8,1024,1024]{1,2,0:T(8,128)}) fusion(bf16[1024,8,64]{0,2,1:T(8,128)(2,1)S(1)} %bitcast.135, bf16[1024,8,64]{0,2,1:T(8,128)(2,1)S(1)} %bitcast.133, pred[1024,1024]{0,1:T(8,128)(4,1)S(1)} %copy-done.15), kind=kOutput, calls=%fused_computation.112 | convolution fusion | flops 1098899456 | bytes 36732928 | tf_op jit(solution)/shard_map/while/body/eval_jaxpr/qhe,khe->hqk/dot_general | solution.py:69
  105.6 13.1 %fusion = f32[8,1024]{1,0:T(8,128)S(1)} fusion(f32[8,1024,1024]{1,2,0:T(8,128)} %get-tuple-element.125, f32[8,1024]{1,0:T(8,128)S(1)} %get-tuple-element.124), kind=kLoop, calls=%fused_computation.6 | loop fusion | flops 16769024 | bytes 33619968 | tf_op jit(solution)/shard_map/while/body/eval_jaxpr/reduce_sum | solution.py:82
  118.8 14.0 %fusion.29 = bf16[8,64,1024]{2,1,0:T(8,128)(2,1)S(1)} fusion(bf16[1024,8,64]{0,2,1:T(8,128)(2,1)S(1)} %bitcast.140, f32[8,1024,1024]{1,2,0:T(8,128)} %get-tuple-element.125, f32[8,1024]{1,0:T(8,128)S(1)} %fusion, f32[8,1024]{1,0:T(8,128)S(1)} %get-tuple-element.124), kind=kOutput, calls=%fused_computation.62 | convolution fusion | flops 1099431936 | bytes 35717120 | tf_op jit(solution)/shard_map/while/body/eval_jaxpr/hqk,khe->qhe/dot_general | solution.py:84
  135.6 11.5 %multiply_convert_fusion.1 = (bf16[1024,2048]{1,0:T(8,128)(2,1)}, f32[1024,2048]{1,0:T(8,128)}) fusion(f32[2048]{0:T(1024)S(1)} %copy-done.46, bf16[512,2048]{1,0:T(8,128)(2,1)} %all-gather.7.cloned.1.call-done, f32[1,1024,512]{1,2,0:T(8,128)} %copy-done.5, f32[512]{0:T(512)S(1)} %copy-done.49, f32[512]{0:T(512)S(1)} %copy-done.43, f32[1024]{0:T(1024)S(1)} %fusion.40, ...), kind=kOutput, calls=%fused_computation.21 | convolution fusion | flops 2171076608 | bytes 16797696 | tf_op jit(solution)/shard_map/nsd,df->nsf/dot_general | solution.py:177
  147.1 10.2 %convert_reduce_fusion = (f32[2048]{0:T(1024)S(1)}, bf16[1024,2048]{1,0:T(8,128)(2,1)S(1)}) fusion(f32[1024,2048]{1,0:T(8,128)} %get-tuple-element.129, f32[2048]{0:T(1024)S(1)} %copy-done.46, bf16[512,2048]{1,0:T(8,128)(2,1)} %all-gather.9.cloned.1.call-done, bf16[1,1024,512]{2,1,0:T(8,128)(2,1)S(1)} %copy-done.24), kind=kOutput, calls=%fused_computation.20 | convolution fusion | flops 2195716096 | bytes 15745024 | tf_op jit(solution)/shard_map/nsd,df->nsf/dot_general | solution.py:184
  157.3 3.7 fusion.62
  161.0 2.9 copy.79
  163.9 3.0 fusion.16
  170.0 1.6 convolution_convert_fusion.4
  171.6 2.0 convolution_convert_fusion.3
  173.6 14.4 %fusion.25 = bf16[8,64,1024]{2,1,0:T(8,128)(2,1)} fusion(bf16[1024,8,64]{0,2,1:T(8,128)(2,1)S(1)} %bitcast.138, f32[8,1024,1024]{1,2,0:T(8,128)} %get-tuple-element.125, f32[8,1024]{1,0:T(8,128)S(1)} %log_add_fusion), kind=kOutput, calls=%fused_computation.59 | convolution fusion | flops 1091043328 | bytes 35684352 | tf_op jit(solution)/shard_map/while/body/eval_jaxpr/hqk,qhe->khe/dot_general | solution.py:96
  188.0 22.0 %multiply_reduce_fusion = (f32[8,1024]{1,0:T(8,128)S(1)}, f32[8,1024,1024]{1,2,0:T(8,128)}) fusion(f32[8,1024,1024]{1,2,0:T(8,128)} %get-tuple-element.125, f32[8,1024]{1,0:T(8,128)S(1)} %log_add_fusion, bf16[1024,8,64]{0,2,1:T(8,128)(2,1)S(1)} %bitcast.139, bf16[1024,8,64]{0,2,1:T(8,128)(2,1)S(1)} %bitcast.141), kind=kOutput, calls=%fused_computation.1 | convolution fusion | flops 1098899456 | bytes 69271552 | tf_op jit(solution)/shard_map/while/body/eval_jaxpr/qhe,khe->hqk/dot_general | solution.py:99
  210.0 28.7 %multiply_convert_fusion = bf16[8,1024,1024]{1,2,0:T(8,128)(2,1)} fusion(f32[8,1024,1024]{1,2,0:T(8,128)} %get-tuple-element.131, f32[8,1024,1024]{1,2,0:T(8,128)} %get-tuple-element.125, f32[8,1024]{1,0:T(8,128)S(1)} %get-tuple-element.130, f32[8,1024]{1,0:T(8,128)S(1)} %log_add_fusion), kind=kLoop, calls=%fused_computation | loop fusion | flops 33554432 | bytes 83951616 | tf_op jit(solution)/shard_map/while/body/eval_jaxpr/convert_element_type | solution.py:103
  238.8 12.1 %multiply_convert_fusion.2 = bf16[8,64,1024]{2,1,0:T(8,128)(2,1)} fusion(bf16[1024,8,64]{0,2,1:T(8,128)(2,1)S(1)} %bitcast.136, bf16[8,1024,1024]{1,2,0:T(8,128)(2,1)} %multiply_convert_fusion), kind=kOutput, calls=%fused_computation.47 | convolution fusion | flops 1074790400 | bytes 18874368 | tf_op jit(solution)/shard_map/while/body/eval_jaxpr/hqk,qhe->khe/dot_general | solution.py:110
  250.8 9.9 %multiply_convert_fusion.3 = bf16[8,64,1024]{2,1,0:T(8,128)(2,1)} fusion(bf16[1024,8,64]{0,2,1:T(8,128)(2,1)S(1)} %bitcast.134, bf16[8,1024,1024]{1,2,0:T(8,128)(2,1)} %multiply_convert_fusion), kind=kOutput, calls=%fused_computation.48 | convolution fusion | flops 1074790400 | bytes 18874368 | tf_op jit(solution)/shard_map/while/body/eval_jaxpr/hqk,khe->qhe/dot_general | solution.py:106
  262.0 2.4 copy.83
  265.8 4.8 fusion.28
  270.6 4.4 copy.89
  275.1 6.6 %convolution_convert_fusion.1 = bf16[512,2048]{1,0:T(8,128)(2,1)} fusion(bf16[1024,2048]{1,0:T(8,128)(2,1)} %copy-done.55, f32[1,1024,512]{1,2,0:T(8,128)} %copy-done.5, f32[512]{0:T(512)S(1)} %copy-done.49, f32[512]{0:T(512)S(1)} %copy-done.43, f32[1024]{0:T(1024)S(1)} %fusion.40, f32[1024]{0:T(1024)S(1)} %broadcast_multiply_fusion), kind=kOutput, calls=%fused_computation.30 | convolution fusion | flops 2151153664 | bytes 8400896 | tf_op jit(solution)/shard_map/nsd,nsf->df/dot_general | solution.py:188
  283.0 6.0 %fusion.15 = bf16[512,2048]{0,1:T(8,128)(2,1)} fusion(bf16[1024,2048]{1,0:T(8,128)(2,1)} %get-tuple-element.128, bf16[1,1024,512]{2,1,0:T(8,128)(2,1)S(1)} %copy-done.25), kind=kOutput, calls=%fused_computation.31 | convolution fusion | flops 2148532224 | bytes 7340032 | tf_op jit(solution)/shard_map/nsd,nsf->df/dot_general | solution.py:183
  289.0 4.0 copy.110
  294.9 4.9 fusion.61
  299.8 2.9 copy.86
  302.7 2.3 fusion.18
  306.8 2.6 fusion.55
  309.5 1.6 copy.108
  311.2 24.4 %all-reduce.3.cloned.1.call-done = bf16[3,512,512]{2,0,1:T(4,128)(2,1)} async-done(((bf16[3,512,512]{2,0,1:T(4,128)(2,1)}), bf16[3,512,512]{2,0,1:T(4,128)(2,1)}) %all-reduce.3.cloned.1.call-update) | async-done | bytes 1572880
  336.6 14.0 %copy.106 = bf16[3,64,512]{0,1,2:T(8,128)(2,1)} copy(bf16[3,64,512]{2,0,1:T(4,128)(2,1)S(1)} %constant_dynamic-slice_fusion) | data formatting | bytes 393216
  350.6 13.9 %reshape.435 = bf16[512,192]{1,0:T(8,128)(2,1)} reshape(bf16[512,64,3]{2,1,0:T(8,128)(2,1)} %bitcast.132) | data formatting | bytes 393216
  364.6 67.5 %all-gather = f32[32,1,1024]{2,1,0:T(1,128)S(1)} all-gather(f32[1,1,1024]{2,1,0:T(1,128)S(1)} %maximum_bitcast_fusion), channel_id=1, replica_groups=mesh['dp'=8,'tensor'=4] {'dp','tensor'}, dimensions={0}, use_global_device_ids=true | all-gather | bytes 135168 | tf_op jit(solution)/shard_map/all_gather | solution.py:215
  433.1 5.2 %fusion.21 = bf16[1,1024,512]{1,2,0:T(8,128)(2,1)S(1)} fusion(f32[1,1024,512]{1,2,0:T(8,128)S(1)} %copy-done.7, bf16[1024,2048]{1,0:T(8,128)(2,1)} %get-tuple-element.128, bf16[512,2048]{1,0:T(8,128)(2,1)} %all-gather.9.cloned.1.call-done, f32[512]{0:T(512)S(1)} %copy-done.50), kind=kOutput, calls=%fused_computation.44 | convolution fusion | flops 2149056512 | bytes 9439232 | tf_op jit(solution)/shard_map/nsf,df->nsd/dot_general | solution.py:180
  438.4 2.1 copy.111
  441.8 22.7 %psum.14 = f32[4608]{0:T(1024)S(1)} all-reduce(f32[4608]{0:T(1024)S(1)} %constant_dynamic-update-slice_fusion), channel_id=1, replica_groups=mesh['dp'=8,'tensor'=4] {'dp'}, use_global_device_ids=true, to_apply=%region_27.28 | all-reduce | flops 4608 | bytes 36864 | tf_op jit(solution)/shard_map/psum | solution.py:15
  464.6 15.8 %psum.15 = f32[4608]{0:T(1024)S(1)} all-reduce(f32[4608]{0:T(1024)S(1)} %psum.14), channel_id=1, replica_groups=mesh['dp'=8,'tensor'=4] {'tensor'}, use_global_device_ids=true, to_apply=%region_28.29 | all-reduce | flops 4608 | bytes 36864 | tf_op jit(solution)/shard_map/psum | solution.py:16
  480.9 1.8 copy.93
  483.3 2.0 fusion.36
  486.8 5.3 %reshape.436 = bf16[128,64,3]{2,1,0:T(8,128)(2,1)S(1)} reshape(bf16[128,192]{1,0:T(8,128)(2,1)} %reduce-scatter.22.cloned.1.call-done) | data formatting | bytes 98304
  492.1 2.2 copy.107
  495.0 1.5 convert_element_type.154
  496.5 12.2 %reduce-scatter.20.cloned.1.call-done = bf16[64,512]{0,1:T(8,128)(2,1)} async-done(((bf16[64,2048]{0,1:T(8,128)(2,1)}), bf16[64,512]{0,1:T(8,128)(2,1)}) %reduce-scatter.20.cloned.1.call-update) | async-done | bytes 65552 | tf_op jit(solution)/shard_map/reduce_scatter | solution.py:149
  508.7 1.6 copy.95
  (192 shorter events, 28.8 us)
Async XLA Ops:
  7.2 74.9 %copy-start = (f32[512,512]{1,0:T(8,128)S(1)}, f32[512,512]{1,0:T(8,128)}, u32[]{:S(2)}) copy-start(f32[512,512]{1,0:T(8,128)} %param.25) | copy-start | bytes 3145732
  7.2 48.7 %copy-start.51 = (s32[4]{0:T(128)S(1)}, s32[4]{0:T(128)}, u32[]{:S(2)}) copy-start(s32[4]{0:T(128)} %param.20) | copy-start | bytes 52
  7.2 50.7 %copy-start.36 = (f32[64,128]{1,0:T(8,128)S(1)}, f32[64,128]{1,0:T(8,128)}, u32[]{:S(2)}) copy-start(f32[64,128]{1,0:T(8,128)} %param.22) | copy-start | bytes 98308
  7.2 74.4 %copy-start.22 = (bf16[1,1024,512]{2,1,0:T(8,128)(2,1)S(1)}, bf16[1,1024,512]{2,1,0:T(8,128)(2,1)}, u32[]{:S(2)}) copy-start(bf16[1,1024,512]{2,1,0:T(8,128)(2,1)} %param.17) | copy-start | bytes 3145732
  7.2 79.6 %all-gather.5.cloned.1.call-start = ((), (), s32[]{:S(2)}) async-start(), calls=%async_computation.7 | async-start | bytes 1769472 | tf_op jit(solution)/shard_map/all_gather | solution.py:145
  23.1 112.4 %all-gather.7.cloned.1.call-start = ((), (), s32[]{:S(2)}) async-start(), calls=%async_computation.8 | async-start | bytes 2359296 | tf_op jit(solution)/shard_map/all_gather | solution.py:145
  39.2 107.8 %all-gather.9.cloned.1.call-start = ((), (), s32[]{:S(2)}) async-start(), calls=%async_computation.9 | async-start | bytes 2359296 | tf_op jit(solution)/shard_map/all_gather | solution.py:145
  55.1 27.6 %copy-start.44 = (f32[512]{0:T(512)S(1)}, f32[512]{0:T(512)}, u32[]{:S(2)}) copy-start(f32[512]{0:T(512)} %param.26) | copy-start | bytes 6148
  55.2 254.3 %reduce-scatter.14.cloned.1.call-start = ((), (), s32[]{:S(2)}) async-start(), calls=%async_computation.10 | async-start | bytes 589824 | tf_op jit(solution)/shard_map/reduce_scatter | solution.py:148
  57.2 25.6 %copy-start.41 = (f32[1,256]{1,0:T(1,128)}, f32[1,256]{1,0:T(1,128)S(1)}, u32[]{:S(2)}) copy-start(f32[1,256]{1,0:T(1,128)S(1)} %get-tuple-element.139) | copy-start | bytes 3076
  57.2 25.6 %copy-start.39 = (f32[1,256]{1,0:T(1,128)}, f32[1,256]{1,0:T(1,128)S(1)}, u32[]{:S(2)}) copy-start(f32[1,256]{1,0:T(1,128)S(1)} %get-tuple-element.138) | copy-start | bytes 3076
  83.1 3.7 copy-start.30
  83.1 3.7 copy-start.37
  83.1 3.7 copy-start.47
  83.5 6.8 %copy-start.34 = (f32[1024]{0:T(1024)}, f32[1024]{0:T(1024)S(1)}, u32[]{:S(2)}) copy-start(f32[1024]{0:T(1024)S(1)} %multiply_reduce_fusion.2) | copy-start | bytes 12292
  84.0 6.3 %copy-start.32 = (f32[1024]{0:T(1024)}, f32[1024]{0:T(1024)S(1)}, u32[]{:S(2)}) copy-start(f32[1024]{0:T(1024)S(1)} %fusion.39) | copy-start | bytes 12292
  84.5 83.5 %copy-start.13 = (bf16[1,1024,512]{1,2,0:T(8,128)(2,1)}, bf16[1,1024,512]{1,2,0:T(8,128)(2,1)S(1)}, u32[]{:S(2)}) copy-start(bf16[1,1024,512]{1,2,0:T(8,128)(2,1)S(1)} %copy.78) | copy-start | bytes 3145732
  90.6 15.0 %copy-start.9 = (bf16[1,1,1024,512]{2,3,0,1:T(8,128)(2,1)}, bf16[1,1,1024,512]{2,3,0,1:T(8,128)(2,1)S(1)}, u32[]{:S(2)}) copy-start(bf16[1,1,1024,512]{2,3,0,1:T(8,128)(2,1)S(1)} %get-tuple-element.115) | copy-start | bytes 3145732
  90.7 15.0 %copy-start.11 = (bf16[1,1,1024,512]{2,3,0,1:T(8,128)(2,1)}, bf16[1,1,1024,512]{2,3,0,1:T(8,128)(2,1)S(1)}, u32[]{:S(2)}) copy-start(bf16[1,1,1024,512]{2,3,0,1:T(8,128)(2,1)S(1)} %get-tuple-element.116) | copy-start | bytes 3145732
  90.7 28.1 %copy-start.17 = (bf16[1,1,1024,512]{2,3,0,1:T(8,128)(2,1)}, bf16[1,1,1024,512]{2,3,0,1:T(8,128)(2,1)S(1)}, u32[]{:S(2)}) copy-start(bf16[1,1,1024,512]{2,3,0,1:T(8,128)(2,1)S(1)} %get-tuple-element.117) | copy-start | bytes 3145732
  118.8 14.1 %copy-start.28 = (bf16[512,512]{1,0:T(8,128)(2,1)S(1)}, bf16[512,512]{1,0:T(8,128)(2,1)}, u32[]{:S(2)}) copy-start(bf16[512,512]{1,0:T(8,128)(2,1)} %all_gather.30) | copy-start | bytes 1572868
  135.5 11.6 %copy-start.24 = (bf16[1,1024,512]{2,1,0:T(8,128)(2,1)S(1)}, bf16[1,1024,512]{2,1,0:T(8,128)(2,1)}, u32[]{:S(2)}) copy-start(bf16[1,1024,512]{2,1,0:T(8,128)(2,1)} %param.33) | copy-start | bytes 3145732
  147.1 10.3 %copy-start.45 = (bf16[512,2048]{1,0:T(8,128)(2,1)S(1)}, bf16[512,2048]{1,0:T(8,128)(2,1)}, u32[]{:S(2)}) copy-start(bf16[512,2048]{1,0:T(8,128)(2,1)} %all-gather.7.cloned.1.call-done) | copy-start | bytes 6291460
  157.3 3.7 copy-start.55
  163.9 3.0 copy-start.6
  163.9 3.5 copy-start.8
  173.6 14.4 %copy-start.18 = (bf16[1,1,1024,512]{2,3,0,1:T(8,128)(2,1)S(1)}, bf16[1,1,1024,512]{2,3,0,1:T(8,128)(2,1)}, u32[]{:S(2)}) copy-start(bf16[1,1,1024,512]{2,3,0,1:T(8,128)(2,1)} %copy-done.17) | copy-start | bytes 3145732
  210.0 125.6 %all-reduce.3.cloned.1.call-start = ((), (), s32[]{:S(2)}) async-start(), calls=%async_computation.17 | async-start | bytes 4194304
  210.0 28.7 %copy-start.12 = (bf16[1,1,1024,512]{2,3,0,1:T(8,128)(2,1)S(1)}, bf16[1,1,1024,512]{2,3,0,1:T(8,128)(2,1)}, u32[]{:S(2)}) copy-start(bf16[1,1,1024,512]{2,3,0,1:T(8,128)(2,1)} %copy-done.11) | copy-start | bytes 3145732
  238.8 12.1 %copy-start.10 = (bf16[1,1,1024,512]{2,3,0,1:T(8,128)(2,1)S(1)}, bf16[1,1,1024,512]{2,3,0,1:T(8,128)(2,1)}, u32[]{:S(2)}) copy-start(bf16[1,1,1024,512]{2,3,0,1:T(8,128)(2,1)} %copy-done.9) | copy-start | bytes 3145732
  250.8 9.9 %copy-start.19 = (bf16[8,64,1024]{2,1,0:T(8,128)(2,1)S(1)}, bf16[8,64,1024]{2,1,0:T(8,128)(2,1)}, u32[]{:S(2)}) copy-start(bf16[8,64,1024]{2,1,0:T(8,128)(2,1)} %fusion.25) | copy-start | bytes 3145732
  260.7 3.7 copy-start.20
  262.0 3.7 copy-start.26
  262.0 3.7 copy-start.31
  262.0 3.7 copy-start.33
  262.0 3.7 copy-start.38
  262.0 3.7 copy-start.48
  275.0 157.7 %reduce-scatter.16.cloned.1.call-start = ((), (), s32[]{:S(2)}) async-start(), calls=%async_computation.11 | async-start | bytes 2359296 | tf_op jit(solution)/shard_map/reduce_scatter | solution.py:148
  281.8 156.6 %reduce-scatter.26.cloned.1.call-start = ((), (), s32[]{:S(2)}) async-start(), calls=%async_computation.16 | async-start | bytes 2359296
  293.0 192.4 %reduce-scatter.24.cloned.1.call-start = ((), (), s32[]{:S(2)}) async-start(), calls=%async_computation.15 | async-start | bytes 163840
  306.8 2.6 copy-start.42
  311.1 175.7 %reduce-scatter.22.cloned.1.call-start = ((), (), s32[]{:S(2)}) async-start(), calls=%async_computation.14 | async-start | bytes 327680
  350.6 82.5 %copy-start.7 = (f32[1,1024,512]{1,2,0:T(8,128)S(1)}, f32[1,1024,512]{1,2,0:T(8,128)}, u32[]{:S(2)}) copy-start(f32[1,1024,512]{1,2,0:T(8,128)} %copy-done.5) | copy-start | bytes 6291460
  350.6 82.5 %copy-start.50 = (f32[512]{0:T(512)S(1)}, f32[512]{0:T(512)}, u32[]{:S(2)}) copy-start(f32[512]{0:T(512)} %param.32) | copy-start | bytes 6148
  364.5 130.5 %reduce-scatter.18.cloned.1.call-start = ((), (), s32[]{:S(2)}) async-start(), calls=%async_computation.12 | async-start | bytes 327680 | tf_op jit(solution)/shard_map/reduce_scatter | solution.py:149
  432.8 75.9 %reduce-scatter.20.cloned.1.call-start = ((), (), s32[]{:S(2)}) async-start(), calls=%async_computation.13 | async-start | bytes 655360 | tf_op jit(solution)/shard_map/reduce_scatter | solution.py:149
  438.3 42.6 %copy-start.16 = (f32[1,1024,512]{1,2,0:T(8,128)S(1)}, f32[1,1024,512]{1,2,0:T(8,128)}, u32[]{:S(2)}) copy-start(f32[1,1024,512]{1,2,0:T(8,128)} %get-tuple-element.112) | copy-start | bytes 6291460
  486.2 24.1 %copy-start.1 = (f32[512,512]{1,0:T(8,128)S(1)}, f32[512,512]{1,0:T(8,128)}, u32[]{:S(2)}) copy-start(f32[512,512]{1,0:T(8,128)} %param.25) | copy-start | bytes 3145732
  (19 other events, 30.9 us)
Sparse Core Ops, SparseCore 0:
  23.3 25.8 all-gather.4
  51.1 28.5 all-gather.6
  81.6 29.2 all-gather.8
  210.1 32.9 reduce-scatter.13
  275.2 60.3 all-reduce.2
  339.1 40.4 reduce-scatter.15
  382.8 41.2 reduce-scatter.25
  427.0 19.2 reduce-scatter.23
  448.5 17.8 reduce-scatter.21
  468.6 17.8 reduce-scatter.17
  488.8 19.7 reduce-scatter.19
